TPU v7x, 32 devices: a whole 2x2x4 slice. The times are simulated.
32 devices in a mesh: loc: 16 (over z, x, core), yr: 2 (over y).
Axes of the slice: x: 2, y: 2, z: 4, core: 2. Of those that a mesh axis runs over, the one named last changes fastest.
Arguments:
- noise: bfloat16 [2, 111, 512, 1024], P(None, None, ('yr', 'loc')), parts along dimension 2, may hold values from -6 to 6
- loc_factor: bfloat16 [1024, 1024], P('loc'), as said below
- age_factor: bfloat16 [111, 111], replicated, as said below
- mean_rate: float32 [4, 111, 1024], P('yr'), parts along dimension 0, may hold values from -7 to -2
- population: float32 [4, 111, 1024], P('yr'), parts along dimension 0, may hold values from 0.1 to 10
- region_of: int32 [1024, 1], replicated, may hold values from 0 to 63
Outputs:
- log_rates: bfloat16 [2, 111, 1024, 512], P(None, None, 'loc', 'yr'), parts along dimension 3
- loc_survival: float32 [2, 1024, 512], P(None, 'loc', 'yr'), parts along dimension 2
- region_survival: float32 [2, 64, 512], P(None, 'loc', 'yr'), parts along dimension 2
There are 2 independent parts, one for each index of `yr`. A program takes and returns all parts, laid end to end along the dimension named above; an argument that names none is the same for every part. Nothing has to cross between parts.
Inputs may be any that keep to these rules, and one draw needn't show every extreme that they name: `region_of`: every region holds at least one location. `loc_factor`: lower triangular with a positive diagonal. `age_factor`: lower triangular with a positive diagonal.
All inputs are finite; a program needn't handle non-finite values.
Results may differ from a plain program's by a relative error of at most 0.006.
Values may be sent and summed in bfloat16 or wider, within the bound.
No kernel may reach another device: no remote copies, remote signals or barrier semaphores. Data moves between devices by JAX's collectives and lax.ppermute only.
A program may use at most 128 MiB of HBM per device.

v0:
```python
import jax
import jax.numpy as jnp
from jax import lax
from jax.sharding import PartitionSpec as P

REGIONS = 64


def survival(rates):
    hazard = jnp.cumsum(rates, axis=1)
    after = jnp.exp(-hazard)
    total = 0.5 + jnp.sum(after, axis=1) - 0.5 * after[:, -1]
    return total / rates.shape[1]


def shards(noise, loc_factor, age_factor, mean_rate, population, region_of):
    highest = lax.Precision.HIGHEST
    regions_all = REGIONS
    spread = jnp.einsum(
        "sark,lk->sarl",
        noise,
        lax.all_gather(loc_factor, "loc", axis=0, tiled=True),
        preferred_element_type=jnp.float32,
    ).astype(jnp.bfloat16)
    mixed = jnp.einsum("ab,sbrl->sarl", age_factor, spread, preferred_element_type=jnp.float32)
    log_section = (mean_rate[:, :, None, :] + mixed).astype(jnp.bfloat16)
    rates = jnp.exp(log_section.astype(jnp.float32))
    onehot = (region_of == jnp.arange(regions_all, dtype=jnp.int32)[None, :]).astype(jnp.float32)
    totals = jnp.einsum("sal,lg->sag", population, onehot, precision=highest)
    weighted = jnp.einsum(
        "sarl,lg->sarg", population[:, :, None, :] * rates, onehot, precision=highest
    )
    region_section = survival(weighted / totals[:, :, None, :])
    region_moved = lax.all_to_all(region_section, "loc", split_axis=2, concat_axis=1, tiled=True)
    region_survival = jnp.transpose(region_moved, (0, 2, 1))
    turned = jnp.transpose(
        lax.all_to_all(log_section, "loc", split_axis=3, concat_axis=2, tiled=True), (0, 1, 3, 2)
    )
    loc_survival = survival(jnp.exp(turned.astype(jnp.float32)))
    return (turned, loc_survival, region_survival)


def solution(mesh):
    placed = (
        P(None, None, ("yr", "loc"), None),
        P("loc", None),
        P(),
        P("yr", None, None),
        P("yr", None, None),
        P(),
    )
    return jax.shard_map(
        shards,
        mesh=mesh,
        in_specs=placed,
        out_specs=(P(None, None, "loc", "yr"), P(None, "loc", "yr"), P(None, "loc", "yr")),
        check_vma=False,
    )
```

profile of v0, /device:TPU:11, one launch (start us, length us, event | category | flops | bytes accessed | tf_op | source)
XLA Modules:
  0.0 370.4 jit_solution(1363313943726732951)
XLA Ops:
  7.2 0.0 copy-start
  7.2 0.0 all-gather.2.cloned.1.call-start
  7.2 0.7 all-gather.2.cloned.1.call-update
  7.9 1.5 copy.50
  9.4 1.5 copy.56
  10.9 2.0 convolution_bitcast_fusion
  12.9 0.0 copy-start.2
  12.9 38.4 %all-gather.2.cloned.1.call-done = bf16[1024,1024]{1,0:T(8,128)(2,1)} async-done(((bf16[64,1024]{1,0:T(8,128)(2,1)}), bf16[1024,1024]{1,0:T(8,128)(2,1)}) %all-gather.2.cloned.1.call-update) | async-done | bytes 2097168 | tf_op jit(solution)/shard_map/all_gather | solution.py:22
  51.3 0.0 copy-done
  51.3 21.3 %fusion = bf16[2,111,16,1024]{3,1,2,0:T(8,128)(2,1)} fusion(f32[2,111,1024]{2,1,0:T(8,128)S(1)} %copy.50, bf16[2,111,16,1024]{3,2,1,0:T(8,128)(2,1)} %param.6, bf16[1024,1024]{1,0:T(8,128)(2,1)} %all-gather.2.cloned.1.call-done, bf16[111,111]{1,0:T(8,128)(2,1)S(1)} %copy-done), kind=kOutput, calls=%fused_computation.1 | convolution fusion | flops 8267464704 | bytes 17580098 | tf_op jit(solution)/shard_map/ab,sbrl->sarl/dot_general | solution.py:25
  72.6 0.0 copy-done.2
  72.6 12.1 %fusion.25 = f32[2,111,16,64]{1,3,2,0:T(8,128)S(1)} fusion(bf16[2,111,16,1024]{3,1,2,0:T(8,128)(2,1)} %fusion, f32[2,111,1024]{2,1,0:T(8,128)S(1)} %copy.56, f32[2,111,64]{1,2,0:T(8,128)S(1)} %convolution_bitcast_fusion, s32[1024]{0:T(1024)S(1)} %bitcast.62), kind=kOutput, calls=%fused_computation.18 | convolution fusion | flops 2800973824 | bytes 9154048 | tf_op jit(solution)/shard_map/sarl,lg->sarg/dot_general | solution.py:30
  84.7 0.9 copy.58
  85.6 36.4 %fusion.44 = f32[2,111,16,64]{3,2,1,0:T(8,128)S(1)} fusion(f32[2,111,16,64]{3,2,1,0:T(8,128)S(1)} %copy.58), kind=kOutput, calls=%fused_computation.36 | output fusion | flops 25006080 | bytes 1818624 | tf_op jit(solution)/shard_map/jit(cumsum)/reduce_window_sum | solution.py:10
  121.9 0.2 fusion.42
  122.2 0.1 copy.59
  122.3 0.7 reshape.17
  123.0 5.7 %all-to-all-start.1 = ((f32[16,1,128]{2,1,0:T(1,128)}), f32[16,1,128]{2,1,0:T(1,128)S(1)}, u32[]{:S(2)}, u32[]{:S(2)}) async-start(f32[16,1,128]{2,1,0:T(1,128)} %reshape.17), calls=%async_computation.1 | async-start | bytes 16384 | tf_op jit(solution)/shard_map/all_to_all | solution.py:34
  128.7 12.3 %copy.52 = bf16[2,111,16,1024]{1,2,0,3:T(8,128)(2,1)} copy(bf16[2,111,16,1024]{3,1,2,0:T(8,128)(2,1)} %fusion) | data formatting | bytes 14548992 | tf_op jit(solution)/shard_map/convert_element_type | solution.py:26
  141.1 0.0 all-to-all-done.1
  141.1 6.0 %all-to-all-start = ((bf16[2,111,16,1024]{1,2,0,3:T(8,128)(2,1)}), bf16[2,111,16,1024]{1,2,0,3:T(8,128)(2,1)}, u32[]{:S(2)}, u32[]{:S(2)}) async-start(bf16[2,111,16,1024]{1,2,0,3:T(8,128)(2,1)} %copy.52), calls=%async_computation | async-start | bytes 16777216 | tf_op jit(solution)/shard_map/all_to_all | solution.py:37
  147.1 0.5 broadcast.27
  147.6 0.7 reduce
  148.3 0.1 reshape.18
  148.4 0.7 all_to_all.33
  149.1 180.3 %all-to-all-done = bf16[2,111,16,1024]{1,2,0,3:T(8,128)(2,1)} async-done(((bf16[2,111,16,1024]{1,2,0,3:T(8,128)(2,1)}), bf16[2,111,16,1024]{1,2,0,3:T(8,128)(2,1)}, u32[]{:S(2)}, u32[]{:S(2)}) %all-to-all-start) | async-done | bytes 7274528 | tf_op jit(solution)/shard_map/all_to_all | solution.py:37
  329.4 9.8 %copy.54 = bf16[2,111,16,16,64]{1,4,3,2,0:T(8,128)(2,1)} copy(bf16[2,111,16,16,64]{1,3,0,4,2:T(8,128)(2,1)} %bitcast.7) | data formatting | bytes 14548992 | tf_op jit(solution)/shard_map/all_to_all | solution.py:37
  339.3 13.5 %copy.55 = bf16[2,111,256,64]{2,3,1,0:T(8,128)(2,1)} copy(bf16[2,111,256,64]{1,3,2,0:T(8,128)(2,1)} %bitcast.54) | data formatting | bytes 14548992 | tf_op jit(solution)/shard_map/all_to_all | solution.py:37
  352.8 0.0 copy-start.1
  352.8 9.1 %fusion.43 = (f32[2,64,256]{2,1,0:T(8,128)S(1)}, f32[2,111,64,256]{3,2,1,0:T(8,128)}) fusion(bf16[2,111,64,256]{3,2,1,0:T(8,128)(2,1)} %bitcast.55), kind=kOutput, calls=%fused_computation.35 | output fusion | flops 410976256 | bytes 21954560 | tf_op jit(solution)/shard_map/jit(cumsum)/reduce_window_sum | solution.py:10
  361.9 1.6 fusion.34
  363.5 0.0 copy-done.1
  (3 shorter events, 0.0 us)
Async XLA Ops:
  7.2 44.1 %copy-start = (bf16[111,111]{1,0:T(8,128)(2,1)S(1)}, bf16[111,111]{1,0:T(8,128)(2,1)}, u32[]{:S(2)}) copy-start(bf16[111,111]{1,0:T(8,128)(2,1)} %param.8) | copy-start | bytes 73930
  7.2 44.1 %all-gather.2.cloned.1.call-start = ((), (), s32[]{:S(2)}) async-start(), calls=%async_computation.2 | async-start | bytes 2228224 | tf_op jit(solution)/shard_map/all_gather | solution.py:22
  12.9 59.7 %copy-start.2 = (s32[1024,1]{0,1:T(1,128)S(1)}, s32[1024,1]{0,1:T(1,128)}, u32[]{:S(2)}) copy-start(s32[1024,1]{0,1:T(1,128)} %param.11) | copy-start | bytes 12292
  123.0 18.0 %all-to-all-start.1 = ((f32[16,1,128]{2,1,0:T(1,128)}), f32[16,1,128]{2,1,0:T(1,128)S(1)}, u32[]{:S(2)}, u32[]{:S(2)}) async-start(f32[16,1,128]{2,1,0:T(1,128)} %reshape.17), calls=%async_computation.1 | async-start | bytes 16384 | tf_op jit(solution)/shard_map/all_to_all | solution.py:34
  141.1 188.4 %all-to-all-start = ((bf16[2,111,16,1024]{1,2,0,3:T(8,128)(2,1)}), bf16[2,111,16,1024]{1,2,0,3:T(8,128)(2,1)}, u32[]{:S(2)}, u32[]{:S(2)}) async-start(bf16[2,111,16,1024]{1,2,0,3:T(8,128)(2,1)} %copy.52), calls=%async_computation | async-start | bytes 16777216 | tf_op jit(solution)/shard_map/all_to_all | solution.py:37
  352.8 10.7 %copy-start.1 = (bf16[111,111]{1,0:T(8,128)(2,1)S(1)}, bf16[111,111]{1,0:T(8,128)(2,1)}, u32[]{:S(2)}) copy-start(bf16[111,111]{1,0:T(8,128)(2,1)} %param.8) | copy-start | bytes 73930
Sparse Core Ops, SparseCore 0:
  10.2 41.0 all-gather.1
where the time goes:
time: 371 us; the launch traced here: 370 us
  waiting for transfers between devices  219 us (59%)
  other arithmetic  48 us (13%)
  local copies, waits for them, and re-layouts  41.7 us (11%)
  matrix products  35.4 us (10%)
  between operations  14.1 us (4%)
  starting transfers between devices  11.7 us (3%)
    all_to_all x1, waiting for transfers between devices, shards(): lax.all_to_all(log_section, 'loc', split_axis=3, concat_axis=2, tiled=True)  180 us
    another operation x2, other arithmetic, survival(): hazard = jnp.cumsum(rates, axis=1)  45.5 us
    all_gather x1, waiting for transfers between devices, shards(): lax.all_gather(loc_factor, 'loc', axis=0, tiled=True)  38.4 us
    all_to_all x2, local copies, waits for them, and re-layouts, shards(): lax.all_to_all(log_section, 'loc', split_axis=3, concat_axis=2, tiled=True)  23.4 us
    dot_general x1, matrix products, shards(): jnp.einsum('ab,sbrl->sarl', age_factor, spread, preferred_element_type=jn...  21.3 us
    convert_element_type x1, local copies, waits for them, and re-layouts, shards(): log_section = (mean_rate[:, :, None, :] + mixed).astype(jnp.bfloat16)  12.3 us
    dot_general x1, matrix products, shards(): jnp.einsum('sarl,lg->sarg', population[:, :, None, :] * rates, onehot, pr...  12.1 us
  transfers between devices with their start and end apart: 3, of which 2 were waited for; matrix products, arithmetic and copies ran while one was open for 5% of the time, Pallas kernels for 0%

commit v1 on v0

--- a/solution.py
+++ b/solution.py
@@ -4,6 +4,22 @@
 from jax.sharding import PartitionSpec as P
 
 REGIONS = 64
+
+
+def build_the_grid(here_x, join_dim, field):
+    long_array = here_x.shape
+    block_now = here_x.reshape(
+        *long_array[:join_dim], field, long_array[join_dim] // field, *long_array[join_dim + 1 :]
+    )
+    raw_out = jnp.moveaxis(block_now, join_dim, 0)
+    return raw_out
+
+
+def build_heaps(patch, d0):
+    answer = list(patch.shape[1:])
+    answer[d0] *= patch.shape[0]
+    all_rows = jnp.moveaxis(patch, 0, d0).reshape(answer)
+    return all_rows
 
 
 def survival(rates):
@@ -31,7 +47,18 @@
         "sarl,lg->sarg", population[:, :, None, :] * rates, onehot, precision=highest
     )
     region_section = survival(weighted / totals[:, :, None, :])
-    region_moved = lax.all_to_all(region_section, "loc", split_axis=2, concat_axis=1, tiled=True)
+    row_out = lax.axis_index("loc")
+    current_arr = lax.axis_size("loc")
+    shaped, state_next = (current_arr, row_out)
+    outer = build_the_grid(region_section, 2, shaped)
+    sheets = [outer[state_next]]
+    for to_i in range(1, shaped):
+        formed = outer[state_next ^ to_i]
+        finding = lax.ppermute(formed, "loc", [(idx, idx ^ to_i) for idx in range(shaped)])
+        sheets.append(finding)
+    lower = jnp.stack(sheets, axis=0)
+    outer = lower[state_next ^ jnp.arange(shaped)]
+    region_moved = build_heaps(outer, 1)
     region_survival = jnp.transpose(region_moved, (0, 2, 1))
     turned = jnp.transpose(
         lax.all_to_all(log_section, "loc", split_axis=3, concat_axis=2, tiled=True), (0, 1, 3, 2)

time: 371 us -> 335 us (0.903); the launches traced: 370 us -> 330 us
  waiting for transfers between devices: 219 us -> 142 us
  starting transfers between devices: 11.7 us -> 50.7 us
    all_to_all x1, waiting for transfers between devices: 180 us -> 0.01 us  [shards(): lax.all_to_all(log_section, 'loc', split_axis=3, concat_axis=2, tiled=True)]
    ppermute x0 -> x15, waiting for transfers between devices: none -> 99.7 us  [shards(): lax.ppermute(formed, 'loc', [(idx, idx ^ to_i) for idx in range(shaped)])]
    ppermute x0 -> x15, starting transfers between devices: none -> 43.7 us  [shards(): lax.ppermute(formed, 'loc', [(idx, idx ^ to_i) for idx in range(shaped)])]
    all_to_all x1 -> x0, starting transfers between devices: 5.68 us -> none  [shards(): lax.all_to_all(region_section, 'loc', split_axis=2, concat_axis=1, tiled=...]
  transfers between devices with their start and end apart: 3 -> 17, of which waited for: 2 -> 11; matrix products, arithmetic and copies ran while one was open for 5% -> 17% of each run, Pallas kernels for 0% -> 0%
where the time goes in v1:
time: 335 us; the launch traced here: 330 us
  waiting for transfers between devices  142 us (42%)
  starting transfers between devices  50.7 us (15%)
  other arithmetic  47.3 us (14%)
  local copies, waits for them, and re-layouts  41 us (12%)
  matrix products  34.3 us (10%)
  between operations  14.2 us (4%)
    ppermute x15, waiting for transfers between devices, shards(): lax.ppermute(formed, 'loc', [(idx, idx ^ to_i) for idx in range(shaped)])  99.7 us
    another operation x2, other arithmetic, survival(): hazard = jnp.cumsum(rates, axis=1)  45.5 us
    ppermute x15, starting transfers between devices, shards(): lax.ppermute(formed, 'loc', [(idx, idx ^ to_i) for idx in range(shaped)])  43.7 us
    all_gather x1, waiting for transfers between devices, shards(): lax.all_gather(loc_factor, 'loc', axis=0, tiled=True)  41.9 us
    all_to_all x2, local copies, waits for them, and re-layouts, shards(): lax.all_to_all(log_section, 'loc', split_axis=3, concat_axis=2, tiled=True)  23.4 us
    dot_general x1, matrix products, shards(): jnp.einsum('ab,sbrl->sarl', age_factor, spread, preferred_element_type=jn...  21.3 us
    convert_element_type x1, local copies, waits for them, and re-layouts, shards(): log_section = (mean_rate[:, :, None, :] + mixed).astype(jnp.bfloat16)  12.4 us
    dot_general x1, matrix products, shards(): jnp.einsum('sarl,lg->sarg', population[:, :, None, :] * rates, onehot, pr...  12.1 us
  transfers between devices with their start and end apart: 17, of which 11 were waited for; matrix products, arithmetic and copies ran while one was open for 17% of the time, Pallas kernels for 0%

profile of v1, /device:TPU:11, one launch (start us, length us, event | category | flops | bytes accessed | tf_op | source)
XLA Modules:
  0.0 329.8 jit_solution(14680733655617433019)
XLA Ops:
  7.2 0.0 copy-start
  7.2 0.0 all-gather.2.cloned.1.call-start
  7.2 0.7 all-gather.2.cloned.1.call-update
  7.9 1.5 copy.53
  9.4 41.9 %all-gather.2.cloned.1.call-done = bf16[1024,1024]{1,0:T(8,128)(2,1)} async-done(((bf16[64,1024]{1,0:T(8,128)(2,1)}), bf16[1024,1024]{1,0:T(8,128)(2,1)}) %all-gather.2.cloned.1.call-update) | async-done | bytes 2097168 | tf_op jit(solution)/shard_map/all_gather | solution.py:38
  51.3 21.3 %fusion = bf16[2,111,16,1024]{3,1,2,0:T(8,128)(2,1)} fusion(f32[2,111,1024]{2,1,0:T(8,128)S(1)} %copy.53, bf16[2,111,16,1024]{3,2,1,0:T(8,128)(2,1)} %param.6, bf16[1024,1024]{1,0:T(8,128)(2,1)} %all-gather.2.cloned.1.call-done, bf16[111,111]{1,0:T(8,128)(2,1)S(1)} %copy-done), kind=kOutput, calls=%fused_computation.2 | convolution fusion | flops 8267464704 | bytes 17580098 | tf_op jit(solution)/shard_map/ab,sbrl->sarl/dot_general | solution.py:41
  72.6 12.4 %copy.55 = bf16[2,111,16,1024]{1,2,0,3:T(8,128)(2,1)} copy(bf16[2,111,16,1024]{3,1,2,0:T(8,128)(2,1)} %fusion) | data formatting | bytes 14548992 | tf_op jit(solution)/shard_map/convert_element_type | solution.py:42
  85.0 6.9 %all-to-all-start = ((bf16[2,111,16,1024]{1,2,0,3:T(8,128)(2,1)}), bf16[2,111,16,1024]{1,2,0,3:T(8,128)(2,1)}, u32[]{:S(2)}, u32[]{:S(2)}) async-start(bf16[2,111,16,1024]{1,2,0,3:T(8,128)(2,1)} %copy.55), calls=%async_computation | async-start | bytes 16777216 | tf_op jit(solution)/shard_map/all_to_all | solution.py:64
  92.0 1.2 copy.59
  93.2 0.9 convolution_bitcast_fusion
  94.0 12.1 %fusion.25 = f32[2,111,16,64]{1,3,2,0:T(8,128)S(1)} fusion(bf16[2,111,16,1024]{3,1,2,0:T(8,128)(2,1)} %fusion, f32[2,111,1024]{2,1,0:T(8,128)} %copy.59, f32[2,111,64]{1,2,0:T(8,128)S(1)} %convolution_bitcast_fusion, s32[1024]{0:T(1024)S(1)} %bitcast.118), kind=kOutput, calls=%fused_computation.19 | convolution fusion | flops 2800973824 | bytes 9154048 | tf_op jit(solution)/shard_map/sarl,lg->sarg/dot_general | solution.py:46
  106.2 0.9 copy.61
  107.0 36.4 %fusion.42 = f32[2,111,16,64]{3,2,1,0:T(8,128)S(1)} fusion(f32[2,111,16,64]{3,2,1,0:T(8,128)S(1)} %copy.61), kind=kOutput, calls=%fused_computation.70 | output fusion | flops 25006080 | bytes 1818624 | tf_op jit(solution)/shard_map/jit(cumsum)/reduce_window_sum | solution.py:26
  143.4 0.2 negate_exponential_fusion.1
  143.7 0.1 copy.62
  143.8 0.1 copy.63
  143.9 0.1 dynamic-slice_bitcast_fusion
  144.0 0.4 collective-permute-start
  144.4 1.2 collective-permute-start.14
  145.7 1.2 collective-permute-start.13
  146.8 1.7 collective-permute-start.12
  148.5 0.3 collective-permute-start.11
  148.8 0.0 collective-permute-done
  148.8 0.3 collective-permute-start.1
  149.1 2.2 collective-permute-done.1
  151.3 1.8 collective-permute-start.2
  153.1 1.3 collective-permute-done.2
  154.4 9.0 %collective-permute-start.3 = (f32[2,16,4]{1,2,0:T(4,128)S(1)}, f32[2,16,4]{1,2,0:T(4,128)S(1)}, u32[]{:S(2)}, u32[]{:S(2)}) collective-permute-start(f32[2,16,4]{1,2,0:T(4,128)S(1)} %get-tuple-element.25), channel_id=1, source_target_pairs={{0,8},{2,10},{4,12},{6,14},{8,0},{10,2},{12,4},{14,6},{16,24},{18,... | collective-permute-start | bytes 1544 | tf_op jit(solution)/shard_map/ppermute | solution.py:57
  163.4 66.4 %collective-permute-done.3 = f32[2,16,4]{1,2,0:T(4,128)S(1)} collective-permute-done((f32[2,16,4]{1,2,0:T(4,128)S(1)}, f32[2,16,4]{1,2,0:T(4,128)S(1)}, u32[]{:S(2)}, u32[]{:S(2)}) %collective-permute-start.3) | collective-permute-done | bytes 544 | tf_op jit(solution)/shard_map/ppermute | solution.py:57
  229.8 0.0 collective-permute-start.4
  229.8 3.0 collective-permute-done.4
  232.8 3.3 %collective-permute-done.5 = f32[2,16,4]{1,2,0:T(4,128)S(1)} collective-permute-done((f32[2,16,4]{1,2,0:T(4,128)S(1)}, f32[2,16,4]{1,2,0:T(4,128)S(1)}, u32[]{:S(2)}, u32[]{:S(2)}) %collective-permute-start.5) | collective-permute-done | bytes 544 | tf_op jit(solution)/shard_map/ppermute | solution.py:57
  236.2 18.4 %collective-permute-start.6 = (f32[2,16,4]{1,2,0:T(4,128)S(1)}, f32[2,16,4]{1,2,0:T(4,128)S(1)}, u32[]{:S(2)}, u32[]{:S(2)}) collective-permute-start(f32[2,16,4]{1,2,0:T(4,128)S(1)} %get-tuple-element.22), channel_id=1, source_target_pairs={{0,14},{2,12},{4,10},{6,8},{8,6},{10,4},{12,2},{14,0},{16,30},{18,... | collective-permute-start | bytes 1544 | tf_op jit(solution)/shard_map/ppermute | solution.py:57
  254.6 1.3 collective-permute-done.6
  255.9 0.0 collective-permute-start.7
  255.9 17.0 %collective-permute-done.7 = f32[2,16,4]{1,2,0:T(4,128)S(1)} collective-permute-done((f32[2,16,4]{1,2,0:T(4,128)S(1)}, f32[2,16,4]{1,2,0:T(4,128)S(1)}, u32[]{:S(2)}, u32[]{:S(2)}) %collective-permute-start.7) | collective-permute-done | bytes 544 | tf_op jit(solution)/shard_map/ppermute | solution.py:57
  272.9 3.9 %collective-permute-start.8 = (f32[2,16,4]{1,2,0:T(4,128)S(1)}, f32[2,16,4]{1,2,0:T(4,128)S(1)}, u32[]{:S(2)}, u32[]{:S(2)}) collective-permute-start(f32[2,16,4]{1,2,0:T(4,128)S(1)} %get-tuple-element.20), channel_id=1, source_target_pairs={{0,18},{2,16},{4,22},{6,20},{8,26},{10,24},{12,30},{14,28},{16,2},... | collective-permute-start | bytes 1544 | tf_op jit(solution)/shard_map/ppermute | solution.py:57
  276.7 1.3 collective-permute-done.8
  278.0 1.7 collective-permute-start.9
  279.7 2.6 collective-permute-done.9
  282.3 3.9 %collective-permute-start.10 = (f32[2,16,4]{1,2,0:T(4,128)S(1)}, f32[2,16,4]{1,2,0:T(4,128)S(1)}, u32[]{:S(2)}, u32[]{:S(2)}) collective-permute-start(f32[2,16,4]{1,2,0:T(4,128)S(1)} %get-tuple-element.18), channel_id=1, source_target_pairs={{0,22},{2,20},{4,18},{6,16},{8,30},{10,28},{12,26},{14,24},{16,6},... | collective-permute-start | bytes 1544 | tf_op jit(solution)/shard_map/ppermute | solution.py:57
  286.2 1.3 collective-permute-done.10
  287.6 0.6 gather_fusion
  288.2 0.7 reshape.68
  288.9 9.9 %copy.57 = bf16[2,111,16,16,64]{1,4,3,2,0:T(8,128)(2,1)} copy(bf16[2,111,16,16,64]{1,3,0,4,2:T(8,128)(2,1)} %bitcast.7) | data formatting | bytes 14548992 | tf_op jit(solution)/shard_map/all_to_all | solution.py:64
  298.8 13.5 %copy.58 = bf16[2,111,256,64]{2,3,1,0:T(8,128)(2,1)} copy(bf16[2,111,256,64]{1,3,2,0:T(8,128)(2,1)} %bitcast.110) | data formatting | bytes 14548992 | tf_op jit(solution)/shard_map/all_to_all | solution.py:64
  312.3 9.1 %fusion.41 = (f32[2,64,256]{2,1,0:T(8,128)S(1)}, f32[2,111,64,256]{3,2,1,0:T(8,128)}) fusion(bf16[2,111,64,256]{3,2,1,0:T(8,128)(2,1)} %bitcast.111), kind=kOutput, calls=%fused_computation.69 | output fusion | flops 410976256 | bytes 21954560 | tf_op jit(solution)/shard_map/jit(cumsum)/reduce_window_sum | solution.py:26
  321.4 1.6 fusion.34
  (35 shorter events, 0.2 us)
Async XLA Ops:
  7.2 44.1 %copy-start = (bf16[111,111]{1,0:T(8,128)(2,1)S(1)}, bf16[111,111]{1,0:T(8,128)(2,1)}, u32[]{:S(2)}) copy-start(bf16[111,111]{1,0:T(8,128)(2,1)} %param.8) | copy-start | bytes 73930
  7.2 44.1 %all-gather.2.cloned.1.call-start = ((), (), s32[]{:S(2)}) async-start(), calls=%async_computation.1 | async-start | bytes 2228224 | tf_op jit(solution)/shard_map/all_gather | solution.py:38
  85.0 6.9 %copy-start.2 = (f32[2,111,1024]{2,0,1:T(2,128)S(1)}, f32[2,111,1024]{2,0,1:T(2,128)}, u32[]{:S(2)}) copy-start(f32[2,111,1024]{2,0,1:T(2,128)} %param.10) | copy-start | bytes 2727940
  85.0 8.2 %copy-start.3 = (s32[1024,1]{0,1:T(1,128)S(1)}, s32[1024,1]{0,1:T(1,128)}, u32[]{:S(2)}) copy-start(s32[1024,1]{0,1:T(1,128)} %param.11) | copy-start | bytes 12292
  85.0 203.9 %all-to-all-start = ((bf16[2,111,16,1024]{1,2,0,3:T(8,128)(2,1)}), bf16[2,111,16,1024]{1,2,0,3:T(8,128)(2,1)}, u32[]{:S(2)}, u32[]{:S(2)}) async-start(bf16[2,111,16,1024]{1,2,0,3:T(8,128)(2,1)} %copy.55), calls=%async_computation | async-start | bytes 16777216 | tf_op jit(solution)/shard_map/all_to_all | solution.py:64
  144.0 4.8 %collective-permute-start = (f32[2,16,4]{1,2,0:T(4,128)S(1)}, f32[2,16,4]{1,2,0:T(4,128)S(1)}, u32[]{:S(2)}, u32[]{:S(2)}) collective-permute-start(f32[2,16,4]{1,2,0:T(4,128)S(1)} %get-tuple-element.28), channel_id=1, source_target_pairs={{0,2},{2,0},{4,6},{6,4},{8,10},{10,8},{12,14},{14,12},{16,18},{18,... | collective-permute-start | bytes 1544 | tf_op jit(solution)/shard_map/ppermute | solution.py:57
  144.4 143.2 %collective-permute-start.14 = (f32[2,16,4]{1,2,0:T(4,128)S(1)}, f32[2,16,4]{1,2,0:T(4,128)S(1)}, u32[]{:S(2)}, u32[]{:S(2)}) collective-permute-start(f32[2,16,4]{1,2,0:T(4,128)S(1)} %get-tuple-element.14), channel_id=1, source_target_pairs={{0,30},{2,28},{4,26},{6,24},{8,22},{10,20},{12,18},{14,16},{16,14}... | collective-permute-start | bytes 1544 | tf_op jit(solution)/shard_map/ppermute | solution.py:57
  145.7 141.9 %collective-permute-start.13 = (f32[2,16,4]{1,2,0:T(4,128)S(1)}, f32[2,16,4]{1,2,0:T(4,128)S(1)}, u32[]{:S(2)}, u32[]{:S(2)}) collective-permute-start(f32[2,16,4]{1,2,0:T(4,128)S(1)} %get-tuple-element.15), channel_id=1, source_target_pairs={{0,28},{2,30},{4,24},{6,26},{8,20},{10,22},{12,16},{14,18},{16,12}... | collective-permute-start | bytes 1544 | tf_op jit(solution)/shard_map/ppermute | solution.py:57
  146.8 140.7 %collective-permute-start.12 = (f32[2,16,4]{1,2,0:T(4,128)S(1)}, f32[2,16,4]{1,2,0:T(4,128)S(1)}, u32[]{:S(2)}, u32[]{:S(2)}) collective-permute-start(f32[2,16,4]{1,2,0:T(4,128)S(1)} %get-tuple-element.16), channel_id=1, source_target_pairs={{0,26},{2,24},{4,30},{6,28},{8,18},{10,16},{12,22},{14,20},{16,10}... | collective-permute-start | bytes 1544 | tf_op jit(solution)/shard_map/ppermute | solution.py:57
  148.5 139.0 %collective-permute-start.11 = (f32[2,16,4]{1,2,0:T(4,128)S(1)}, f32[2,16,4]{1,2,0:T(4,128)S(1)}, u32[]{:S(2)}, u32[]{:S(2)}) collective-permute-start(f32[2,16,4]{1,2,0:T(4,128)S(1)} %get-tuple-element.17), channel_id=1, source_target_pairs={{0,24},{2,26},{4,28},{6,30},{8,16},{10,18},{12,20},{14,22},{16,8},... | collective-permute-start | bytes 1544 | tf_op jit(solution)/shard_map/ppermute | solution.py:57
  148.8 2.5 collective-permute-start.1
  151.3 3.1 collective-permute-start.2
  154.4 75.4 %collective-permute-start.3 = (f32[2,16,4]{1,2,0:T(4,128)S(1)}, f32[2,16,4]{1,2,0:T(4,128)S(1)}, u32[]{:S(2)}, u32[]{:S(2)}) collective-permute-start(f32[2,16,4]{1,2,0:T(4,128)S(1)} %get-tuple-element.25), channel_id=1, source_target_pairs={{0,8},{2,10},{4,12},{6,14},{8,0},{10,2},{12,4},{14,6},{16,24},{18,... | collective-permute-start | bytes 1544 | tf_op jit(solution)/shard_map/ppermute | solution.py:57
  229.8 3.0 collective-permute-start.4
  232.8 3.4 %collective-permute-start.5 = (f32[2,16,4]{1,2,0:T(4,128)S(1)}, f32[2,16,4]{1,2,0:T(4,128)S(1)}, u32[]{:S(2)}, u32[]{:S(2)}) collective-permute-start(f32[2,16,4]{1,2,0:T(4,128)S(1)} %get-tuple-element.23), channel_id=1, source_target_pairs={{0,12},{2,14},{4,8},{6,10},{8,4},{10,6},{12,0},{14,2},{16,28},{18,... | collective-permute-start | bytes 1544 | tf_op jit(solution)/shard_map/ppermute | solution.py:57
  236.2 19.7 %collective-permute-start.6 = (f32[2,16,4]{1,2,0:T(4,128)S(1)}, f32[2,16,4]{1,2,0:T(4,128)S(1)}, u32[]{:S(2)}, u32[]{:S(2)}) collective-permute-start(f32[2,16,4]{1,2,0:T(4,128)S(1)} %get-tuple-element.22), channel_id=1, source_target_pairs={{0,14},{2,12},{4,10},{6,8},{8,6},{10,4},{12,2},{14,0},{16,30},{18,... | collective-permute-start | bytes 1544 | tf_op jit(solution)/shard_map/ppermute | solution.py:57
  255.9 17.0 %collective-permute-start.7 = (f32[2,16,4]{1,2,0:T(4,128)S(1)}, f32[2,16,4]{1,2,0:T(4,128)S(1)}, u32[]{:S(2)}, u32[]{:S(2)}) collective-permute-start(f32[2,16,4]{1,2,0:T(4,128)S(1)} %get-tuple-element.21), channel_id=1, source_target_pairs={{0,16},{2,18},{4,20},{6,22},{8,24},{10,26},{12,28},{14,30},{16,0},... | collective-permute-start | bytes 1544 | tf_op jit(solution)/shard_map/ppermute | solution.py:57
  272.9 5.1 %collective-permute-start.8 = (f32[2,16,4]{1,2,0:T(4,128)S(1)}, f32[2,16,4]{1,2,0:T(4,128)S(1)}, u32[]{:S(2)}, u32[]{:S(2)}) collective-permute-start(f32[2,16,4]{1,2,0:T(4,128)S(1)} %get-tuple-element.20), channel_id=1, source_target_pairs={{0,18},{2,16},{4,22},{6,20},{8,26},{10,24},{12,30},{14,28},{16,2},... | collective-permute-start | bytes 1544 | tf_op jit(solution)/shard_map/ppermute | solution.py:57
  278.0 4.3 %collective-permute-start.9 = (f32[2,16,4]{1,2,0:T(4,128)S(1)}, f32[2,16,4]{1,2,0:T(4,128)S(1)}, u32[]{:S(2)}, u32[]{:S(2)}) collective-permute-start(f32[2,16,4]{1,2,0:T(4,128)S(1)} %get-tuple-element.19), channel_id=1, source_target_pairs={{0,20},{2,22},{4,16},{6,18},{8,28},{10,30},{12,24},{14,26},{16,4},... | collective-permute-start | bytes 1544 | tf_op jit(solution)/shard_map/ppermute | solution.py:57
  282.3 5.2 %collective-permute-start.10 = (f32[2,16,4]{1,2,0:T(4,128)S(1)}, f32[2,16,4]{1,2,0:T(4,128)S(1)}, u32[]{:S(2)}, u32[]{:S(2)}) collective-permute-start(f32[2,16,4]{1,2,0:T(4,128)S(1)} %get-tuple-element.18), channel_id=1, source_target_pairs={{0,22},{2,20},{4,18},{6,16},{8,30},{10,28},{12,26},{14,24},{16,6},... | collective-permute-start | bytes 1544 | tf_op jit(solution)/shard_map/ppermute | solution.py:57
  312.3 10.7 %copy-start.1 = (bf16[111,111]{1,0:T(8,128)(2,1)S(1)}, bf16[111,111]{1,0:T(8,128)(2,1)}, u32[]{:S(2)}) copy-start(bf16[111,111]{1,0:T(8,128)(2,1)} %param.8) | copy-start | bytes 73930
Sparse Core Ops, SparseCore 0:
  10.2 41.0 all-gather.1
